TPU v7x, 32 devices: a whole 2x2x4 slice. The times are simulated.
32 devices in a mesh: dp: 4 (over x, core), expert: 8 (over z, y).
Axes of the slice: x: 2, y: 2, z: 4, core: 2. Of those that a mesh axis runs over, the one named last changes fastest.
Arguments:
- tokens: bfloat16 [4096, 4096], P(('dp', 'expert')), may hold values from -6 to 6
- router: bfloat16 [4096, 8], replicated, may hold values from -0.09375 to 0.09375
- price: float32 [8], replicated, may hold values from -1 to 1
- w_in: bfloat16 [8, 4096, 8192], P('expert', None, 'dp'), may hold values from -0.09375 to 0.09375
- w_out: bfloat16 [8, 8192, 4096], P('expert', 'dp'), may hold values from -0.0625 to 0.0625
- assign: int32 [4096], P(('dp', 'expert')), may hold values from 0 to 7, as said below
Outputs:
- mixed: bfloat16 [4096, 4096], P(('dp', 'expert'))
- new_price: float32 [8], replicated
Inputs may be any that keep to these rules, and one draw needn't show every extreme that they name: `assign`: every expert is named by exactly 512 tokens in all, and by at most 24 of the 128 tokens of one device (aligned blocks of 128 rows); on every device some expert is named exactly 24 times, and the experts' loads on one device are, in some order, the same 8 numbers on every device.
All inputs are finite; a program needn't handle non-finite values.
Results may differ from a plain program's by a relative error of at most 0.013.
Values may be sent and summed in bfloat16 or wider, within the bound.
A program may use at most 128 MiB of HBM per device.

v0:
```python
import jax
import jax.numpy as jnp
from jax import lax
from jax.sharding import PartitionSpec as P

BID_STEP = 0.01


def shards(tokens, router, price, w_in, w_out, assign):
    experts = router.shape[1]
    width = tokens.shape[1]
    local_tokens = tokens.shape[0]
    capacity = 3 * local_tokens // (2 * experts)
    first = w_in[0]
    second = w_out[0]
    affinity = jnp.dot(tokens, router, preferred_element_type=jnp.float32)
    onehot = assign[:, None] == jnp.arange(experts, dtype=jnp.int32)[None, :]
    own = jnp.sum(jnp.where(onehot, affinity, 0.0), axis=1)
    rival = jnp.max(jnp.where(onehot, -1e30, affinity - price[None, :]), axis=1)
    bid = own - rival + BID_STEP
    local_best = jnp.max(jnp.where(onehot, bid[:, None], -1e30), axis=0)
    new_price = lax.pmax(local_best, ("dp", "expert"))
    lower = (jnp.arange(local_tokens)[:, None] >= jnp.arange(local_tokens)[None, :]).astype(
        jnp.bfloat16
    )
    running = jnp.dot(lower, onehot.astype(jnp.bfloat16), preferred_element_type=jnp.float32)
    slots = jnp.sum(jnp.where(onehot, running, 0.0), axis=1).astype(jnp.int32) - 1
    place = assign * capacity + slots
    pack = (place[None, :] == jnp.arange(experts * capacity, dtype=jnp.int32)[:, None]).astype(
        jnp.bfloat16
    )
    packed = jnp.dot(pack, tokens, preferred_element_type=jnp.float32).astype(jnp.bfloat16)
    mine = lax.all_to_all(
        packed.reshape(experts, capacity, width), "expert", split_axis=0, concat_axis=0, tiled=True
    )
    rows = lax.all_gather(mine.reshape(experts * capacity, width), "dp", axis=0, tiled=True)
    raw = jnp.dot(rows, first, preferred_element_type=jnp.float32)
    hidden = jax.nn.gelu(raw, approximate=True).astype(jnp.bfloat16)
    partial = jnp.dot(hidden, second, preferred_element_type=jnp.float32).astype(jnp.bfloat16)
    summed = lax.psum_scatter(partial, "dp", scatter_dimension=0, tiled=True)
    returned = lax.all_to_all(
        summed.reshape(experts, capacity, width), "expert", split_axis=0, concat_axis=0, tiled=True
    ).reshape(experts * capacity, width)
    picked = lax.dot_general(
        pack, returned, (((0,), (0,)), ((), ())), preferred_element_type=jnp.float32
    )
    gate = jax.nn.sigmoid(own)
    mixed = (gate[:, None] * picked).astype(jnp.bfloat16)
    return (mixed, new_price)


def solution(mesh):
    return jax.shard_map(
        shards,
        mesh=mesh,
        in_specs=(
            P(("dp", "expert"), None),
            P(),
            P(),
            P("expert", None, "dp"),
            P("expert", "dp", None),
            P(("dp", "expert")),
        ),
        out_specs=(P(("dp", "expert"), None), P()),
        check_vma=False,
    )
```

profile of v0, /device:TPU:0, one launch (start us, length us, event | category | flops | bytes accessed | tf_op | source)
XLA Modules:
  0.0 268.7 jit_solution(14354729918108742788)
XLA Ops:
  7.2 0.0 copy-start
  7.2 0.0 all-gather.2.cloned.1.call-start
  7.2 0.9 fusion.21
  8.1 0.7 add_add_fusion
  8.8 0.0 copy-done
  8.8 0.0 copy-start.2
  8.8 0.6 convolution_convert_fusion
  9.4 44.2 %all_to_all.10 = bf16[8,24,4096]{2,1,0:T(8,128)(2,1)} all-to-all(bf16[8,24,4096]{2,1,0:T(8,128)(2,1)S(1)} %bitcast.23), channel_id=1, replica_groups=mesh['dp'=4,'expert'=8] {'expert'}, dimensions={0} | all-to-all | bytes 3145728 | tf_op jit(solution)/shard_map/all_to_all | solution.py:33
  53.6 0.0 copy-done.2
  53.6 0.0 all-gather.2.cloned.1.call-update
  53.6 0.0 reduce-scatter.2.cloned.1.call-start
  53.6 45.5 %all-gather.2.cloned.1.call-done = bf16[768,4096]{1,0:T(8,128)(2,1)} async-done(((bf16[192,4096]{1,0:T(8,128)(2,1)}), bf16[768,4096]{1,0:T(8,128)(2,1)}) %all-gather.2.cloned.1.call-update) | async-done | bytes 6291472 | tf_op jit(solution)/shard_map/all_gather | solution.py:36
  99.1 40.2 %fusion.4 = bf16[768,4096]{1,0:T(8,128)(2,1)} fusion(bf16[1,2048,4096]{2,1,0:T(8,128)(2,1)} %param.10, bf16[768,4096]{1,0:T(8,128)(2,1)} %all-gather.2.cloned.1.call-done, bf16[1,4096,2048]{2,1,0:T(8,128)(2,1)} %param.9), kind=kOutput, calls=%fused_computation.5 | convolution fusion | flops 25787105280 | bytes 46137344 | tf_op jit(solution)/shard_map/dot_general | solution.py:39
  139.4 0.0 copy-start.1
  139.4 0.0 copy-start.4
  139.4 0.0 copy-start.5
  139.4 0.0 copy-start.3
  139.4 0.0 reduce-scatter.2.cloned.1.call-update
  139.4 58.5 %reduce-scatter.2.cloned.1.call-done = bf16[192,4096]{1,0:T(8,128)(2,1)} async-done(((bf16[768,4096]{1,0:T(8,128)(2,1)}), bf16[192,4096]{1,0:T(8,128)(2,1)}) %reduce-scatter.2.cloned.1.call-update) | async-done | bytes 1572880 | tf_op jit(solution)/shard_map/reduce_scatter | solution.py:40
  197.9 5.5 %all-to-all-start.1 = ((bf16[8,24,4096]{2,1,0:T(8,128)(2,1)}), bf16[8,24,4096]{2,1,0:T(8,128)(2,1)S(1)}, u32[]{:S(2)}, u32[]{:S(2)}) async-start(bf16[8,24,4096]{2,1,0:T(8,128)(2,1)} %bitcast.24), calls=%async_computation.2 | async-start | bytes 3145728 | tf_op jit(solution)/shard_map/all_to_all | solution.py:41
  203.5 0.0 copy-done.1
  203.5 0.0 copy-done.4
  203.5 0.0 copy-done.5
  203.5 0.4 select_reduce_fusion.1
  203.9 0.1 select_reduce_fusion
  204.0 56.3 %pmax.7 = f32[8]{0:T(128)} all-reduce(f32[8]{0:T(128)S(1)} %select_reduce_fusion), channel_id=1, replica_groups=mesh['dp'=4,'expert'=8] {'dp','expert'}, use_global_device_ids=true, to_apply=%region_5.6 | all-reduce | flops 8 | bytes 64 | tf_op jit(solution)/shard_map/pmax | solution.py:22
  260.3 0.0 all-to-all-done.1
  260.3 0.0 copy-done.3
  260.3 1.5 fusion.15
  (1 shorter events, 0.0 us)
Async XLA Ops:
  7.2 1.6 copy-start
  7.2 92.0 %all-gather.2.cloned.1.call-start = ((), (), s32[]{:S(2)}) async-start(), calls=%async_computation.3 | async-start | bytes 7864320 | tf_op jit(solution)/shard_map/all_gather | solution.py:36
  8.8 44.8 %copy-start.2 = (s32[128]{0:T(128)}, s32[128]{0:T(128)S(1)}, u32[]{:S(2)}) copy-start(s32[128]{0:T(128)S(1)} %add_add_fusion) | copy-start | bytes 1540
  53.6 144.3 %reduce-scatter.2.cloned.1.call-start = ((), (), s32[]{:S(2)}) async-start(), calls=%async_computation.4 | async-start | bytes 7864320 | tf_op jit(solution)/shard_map/reduce_scatter | solution.py:40
  139.4 64.1 %copy-start.1 = (bf16[4096,8]{0,1:T(8,128)(2,1)S(1)}, bf16[4096,8]{0,1:T(8,128)(2,1)}, u32[]{:S(2)}) copy-start(bf16[4096,8]{0,1:T(8,128)(2,1)} %param.7) | copy-start | bytes 196612
  139.4 64.1 %copy-start.4 = (f32[8]{0:T(128)S(1)}, f32[8]{0:T(128)}, u32[]{:S(2)}) copy-start(f32[8]{0:T(128)} %param.8) | copy-start | bytes 100
  139.4 64.1 %copy-start.5 = (s32[128]{0:T(128)S(1)}, s32[128]{0:T(128)}, u32[]{:S(2)}) copy-start(s32[128]{0:T(128)} %param.11) | copy-start | bytes 1540
  139.4 121.0 %copy-start.3 = (s32[128]{0:T(128)S(1)}, s32[128]{0:T(128)}, u32[]{:S(2)}) copy-start(s32[128]{0:T(128)} %copy-done.2) | copy-start | bytes 1540
  197.9 62.4 %all-to-all-start.1 = ((bf16[8,24,4096]{2,1,0:T(8,128)(2,1)}), bf16[8,24,4096]{2,1,0:T(8,128)(2,1)S(1)}, u32[]{:S(2)}, u32[]{:S(2)}) async-start(bf16[8,24,4096]{2,1,0:T(8,128)(2,1)} %bitcast.24), calls=%async_computation.2 | async-start | bytes 3145728 | tf_op jit(solution)/shard_map/all_to_all | solution.py:41
Sparse Core Ops, SparseCore 0:
  53.7 45.3 all-gather.1
  139.5 58.3 reduce-scatter.1
where the time goes:
time: 269 us
  waiting for transfers between devices  104 us (39%)
  blocking collectives  101 us (38%)
  matrix products  43.6 us (16%)
  between operations  14.1 us (5%)
  starting transfers between devices  5.59 us (2%)
    reduce_scatter x1, waiting for transfers between devices, shards(): summed = lax.psum_scatter(partial, 'dp', scatter_dimension=0, tiled=True)  58.5 us
    pmax x1, blocking collectives, shards(): new_price = lax.pmax(local_best, ('dp', 'expert'))  56.3 us
    all_gather x1, waiting for transfers between devices, shards(): lax.all_gather(mine.reshape(experts * capacity, width), 'dp', axis=0, til...  45.5 us
    all_to_all x1, blocking collectives, shards(): lax.all_to_all(packed.reshape(experts, capacity, width), 'expert', split_...  44.2 us
    dot_general x1, matrix products, shards(): jnp.dot(hidden, second, preferred_element_type=jnp.float32)  40.2 us
    all_to_all x1, starting transfers between devices, shards(): lax.all_to_all(summed.reshape(experts, capacity, width), 'expert', split_...  5.51 us
  transfers between devices with their start and end apart: 3, of which 2 were waited for; matrix products, arithmetic and copies ran while one was open for 0% of the time, Pallas kernels for 0%

commit v1 on v0

--- a/solution.py
+++ b/solution.py
@@ -4,6 +4,29 @@
 from jax.sharding import PartitionSpec as P
 
 BID_STEP = 0.01
+
+
+def split_up(x, dim, size):
+    shape = x.shape
+    tiles = x.reshape(*shape[:dim], size, shape[dim] // size, *shape[dim + 1 :])
+    return jnp.moveaxis(tiles, dim, 0)
+
+
+def laid_out(parts, dim):
+    parts = jnp.moveaxis(parts, 0, dim)
+    shape = parts.shape
+    return parts.reshape(*shape[:dim], shape[dim] * shape[dim + 1], *shape[dim + 2 :])
+
+
+def exchange_directly(x, axis, split_dim, concat_dim):
+    length, position = (lax.axis_size(axis), lax.axis_index(axis))
+    blocks = split_up(x, split_dim, length)
+    outs = [blocks[position]]
+    for step in range(1, length):
+        sent = blocks[(position + step) % length]
+        outs.append(lax.ppermute(sent, axis, [(i, (i + step) % length) for i in range(length)]))
+    blocks = jnp.stack(outs)[(position - jnp.arange(length)) % length]
+    return laid_out(blocks, concat_dim)
 
 
 def shards(tokens, router, price, w_in, w_out, assign):
@@ -38,9 +61,9 @@
     hidden = jax.nn.gelu(raw, approximate=True).astype(jnp.bfloat16)
     partial = jnp.dot(hidden, second, preferred_element_type=jnp.float32).astype(jnp.bfloat16)
     summed = lax.psum_scatter(partial, "dp", scatter_dimension=0, tiled=True)
-    returned = lax.all_to_all(
-        summed.reshape(experts, capacity, width), "expert", split_axis=0, concat_axis=0, tiled=True
-    ).reshape(experts * capacity, width)
+    returned = exchange_directly(summed.reshape(experts, capacity, width), "expert", 0, 0).reshape(
+        experts * capacity, width
+    )
     picked = lax.dot_general(
         pack, returned, (((0,), (0,)), ((), ())), preferred_element_type=jnp.float32
     )

time: 269 us -> 249 us (0.926)
  the two profiles are of different devices: /device:TPU:0 before, /device:TPU:13 now
where the time goes in v1:
time: 249 us
  waiting for transfers between devices  98.4 us (40%)
  blocking collectives  78.8 us (32%)
  matrix products  43.6 us (18%)
  between operations  14.2 us (6%)
  starting transfers between devices  7.25 us (3%)
  local copies, waits for them, and re-layouts  5.73 us (2%)
    all_gather x1, waiting for transfers between devices, shards(): lax.all_gather(mine.reshape(experts * capacity, width), 'dp', axis=0, til...  49.1 us
    dot_general x1, matrix products, shards(): jnp.dot(hidden, second, preferred_element_type=jnp.float32)  40.3 us
    all_to_all x1, blocking collectives, shards(): lax.all_to_all(packed.reshape(experts, capacity, width), 'expert', split_...  39.4 us
    pmax x1, blocking collectives, shards(): new_price = lax.pmax(local_best, ('dp', 'expert'))  39.4 us
    ppermute x7, waiting for transfers between devices, exchange_directly(): lax.ppermute(sent, axis, [(i, (i + step) % length) for i in range(length)])  31.2 us
    reduce_scatter x1, waiting for transfers between devices, shards(): summed = lax.psum_scatter(partial, 'dp', scatter_dimension=0, tiled=True)  18 us
    ppermute x7, starting transfers between devices, exchange_directly(): lax.ppermute(sent, axis, [(i, (i + step) % length) for i in range(length)])  7.17 us
  transfers between devices with their start and end apart: 9, of which 7 were waited for; matrix products, arithmetic and copies ran while one was open for 0% of the time, Pallas kernels for 0%

profile of v1, /device:TPU:13, one launch (start us, length us, event | category | flops | bytes accessed | tf_op | source)
XLA Modules:
  0.0 248.8 jit_solution(2362474822837224471)
XLA Ops:
  7.2 0.0 copy-start
  7.2 0.0 all-gather.2.cloned.1.call-start
  7.2 0.9 fusion.21
  8.1 0.7 add_add_fusion
  8.8 0.6 convolution_convert_fusion
  9.4 39.4 %all_to_all.5 = bf16[8,24,4096]{2,1,0:T(8,128)(2,1)} all-to-all(bf16[8,24,4096]{2,1,0:T(8,128)(2,1)S(1)} %bitcast.53), channel_id=1, replica_groups=mesh['dp'=4,'expert'=8] {'expert'}, dimensions={0} | all-to-all | bytes 3145728 | tf_op jit(solution)/shard_map/all_to_all | solution.py:56
  48.8 0.0 all-gather.2.cloned.1.call-update
  48.8 0.0 reduce-scatter.2.cloned.1.call-start
  48.9 49.1 %all-gather.2.cloned.1.call-done = bf16[768,4096]{1,0:T(8,128)(2,1)} async-done(((bf16[192,4096]{1,0:T(8,128)(2,1)}), bf16[768,4096]{1,0:T(8,128)(2,1)}) %all-gather.2.cloned.1.call-update) | async-done | bytes 6291472 | tf_op jit(solution)/shard_map/all_gather | solution.py:59
  98.0 40.3 %fusion.4 = bf16[768,4096]{1,0:T(8,128)(2,1)} fusion(bf16[1,2048,4096]{2,1,0:T(8,128)(2,1)} %param.10, bf16[768,4096]{1,0:T(8,128)(2,1)} %all-gather.2.cloned.1.call-done, bf16[1,4096,2048]{2,1,0:T(8,128)(2,1)} %param.9), kind=kOutput, calls=%fused_computation.6 | convolution fusion | flops 25787105280 | bytes 46137344 | tf_op jit(solution)/shard_map/dot_general | solution.py:62
  138.2 0.0 reduce-scatter.2.cloned.1.call-update
  138.3 0.8 copy-done.2
  139.1 0.4 select_reduce_fusion.1
  139.5 0.1 select_reduce_fusion
  139.6 39.4 %pmax.7 = f32[8]{0:T(128)} all-reduce(f32[8]{0:T(128)S(1)} %select_reduce_fusion), channel_id=1, replica_groups=mesh['dp'=4,'expert'=8] {'dp','expert'}, use_global_device_ids=true, to_apply=%region_5.6 | all-reduce | flops 8 | bytes 64 | tf_op jit(solution)/shard_map/pmax | solution.py:45
  179.0 18.0 %reduce-scatter.2.cloned.1.call-done = bf16[192,4096]{1,0:T(8,128)(2,1)} async-done(((bf16[768,4096]{1,0:T(8,128)(2,1)}), bf16[192,4096]{1,0:T(8,128)(2,1)}) %reduce-scatter.2.cloned.1.call-update) | async-done | bytes 1572880 | tf_op jit(solution)/shard_map/reduce_scatter | solution.py:63
  197.1 1.6 dynamic-slice_bitcast_fusion
  198.7 1.2 collective-permute-start
  199.9 1.3 collective-permute-start.1
  201.2 1.1 collective-permute-start.2
  202.3 1.2 collective-permute-start.3
  203.6 1.1 collective-permute-start.4
  204.7 1.2 collective-permute-start.5
  205.9 2.8 %collective-permute-done.1 = bf16[1,24,4096]{2,1,0:T(8,128)(2,1)S(1)} collective-permute-done((bf16[1,24,4096]{2,1,0:T(8,128)(2,1)S(1)}, bf16[1,24,4096]{2,1,0:T(8,128)(2,1)S(1)}, u32[]{:S(2)}, u32[]{:S(2)}) %collective-permute-start.1) | collective-permute-done | bytes 196640 | tf_op jit(solution)/shard_map/ppermute | solution.py:27
  208.7 20.1 %collective-permute-done.2 = bf16[1,24,4096]{2,1,0:T(8,128)(2,1)S(1)} collective-permute-done((bf16[1,24,4096]{2,1,0:T(8,128)(2,1)S(1)}, bf16[1,24,4096]{2,1,0:T(8,128)(2,1)S(1)}, u32[]{:S(2)}, u32[]{:S(2)}) %collective-permute-start.2) | collective-permute-done | bytes 196640 | tf_op jit(solution)/shard_map/ppermute | solution.py:27
  228.8 4.2 %collective-permute-done.3 = bf16[1,24,4096]{2,1,0:T(8,128)(2,1)S(1)} collective-permute-done((bf16[1,24,4096]{2,1,0:T(8,128)(2,1)S(1)}, bf16[1,24,4096]{2,1,0:T(8,128)(2,1)S(1)}, u32[]{:S(2)}, u32[]{:S(2)}) %collective-permute-start.3) | collective-permute-done | bytes 196640 | tf_op jit(solution)/shard_map/ppermute | solution.py:27
  233.0 0.0 copy-start.4
  233.0 2.9 %collective-permute-done.5 = bf16[1,24,4096]{2,1,0:T(8,128)(2,1)S(1)} collective-permute-done((bf16[1,24,4096]{2,1,0:T(8,128)(2,1)S(1)}, bf16[1,24,4096]{2,1,0:T(8,128)(2,1)S(1)}, u32[]{:S(2)}, u32[]{:S(2)}) %collective-permute-start.5) | collective-permute-done | bytes 196640 | tf_op jit(solution)/shard_map/ppermute | solution.py:27
  236.0 1.2 collective-permute-done.6
  237.2 1.1 copy-done.1
  238.4 2.1 gather_fusion
  240.5 1.5 fusion.15
  (23 shorter events, 0.2 us)
Async XLA Ops:
  7.2 1.6 copy-start
  7.2 90.8 %all-gather.2.cloned.1.call-start = ((), (), s32[]{:S(2)}) async-start(), calls=%async_computation.2 | async-start | bytes 7864320 | tf_op jit(solution)/shard_map/all_gather | solution.py:59
  8.8 40.0 %copy-start.3 = (s32[128]{0:T(128)}, s32[128]{0:T(128)S(1)}, u32[]{:S(2)}) copy-start(s32[128]{0:T(128)S(1)} %add_add_fusion) | copy-start | bytes 1540
  48.8 148.2 %reduce-scatter.2.cloned.1.call-start = ((), (), s32[]{:S(2)}) async-start(), calls=%async_computation.3 | async-start | bytes 7864320 | tf_op jit(solution)/shard_map/reduce_scatter | solution.py:63
  138.2 0.8 copy-start.2
  138.2 0.8 copy-start.5
  138.2 0.8 copy-start.6
  198.7 6.0 %collective-permute-start = (bf16[1,24,4096]{2,1,0:T(8,128)(2,1)S(1)}, bf16[1,24,4096]{2,1,0:T(8,128)(2,1)S(1)}, u32[]{:S(2)}, u32[]{:S(2)}) collective-permute-start(bf16[1,24,4096]{2,1,0:T(8,128)(2,1)S(1)} %get-tuple-element.10), channel_id=1, source_target_pairs={{0,1},{1,2},{2,3},{3,4},{4,5},{5,6},{6,7},{7,0},{8,9},{9,10},{10,1... | collective-permute-start | bytes 589832 | tf_op jit(solution)/shard_map/ppermute | solution.py:27
  199.9 8.8 %collective-permute-start.1 = (bf16[1,24,4096]{2,1,0:T(8,128)(2,1)S(1)}, bf16[1,24,4096]{2,1,0:T(8,128)(2,1)S(1)}, u32[]{:S(2)}, u32[]{:S(2)}) collective-permute-start(bf16[1,24,4096]{2,1,0:T(8,128)(2,1)S(1)} %get-tuple-element.9), channel_id=1, source_target_pairs={{0,2},{1,3},{2,4},{3,5},{4,6},{5,7},{6,0},{7,1},{8,10},{9,11},{10,... | collective-permute-start | bytes 589832 | tf_op jit(solution)/shard_map/ppermute | solution.py:27
  201.2 27.6 %collective-permute-start.2 = (bf16[1,24,4096]{2,1,0:T(8,128)(2,1)S(1)}, bf16[1,24,4096]{2,1,0:T(8,128)(2,1)S(1)}, u32[]{:S(2)}, u32[]{:S(2)}) collective-permute-start(bf16[1,24,4096]{2,1,0:T(8,128)(2,1)S(1)} %get-tuple-element.8), channel_id=1, source_target_pairs={{0,3},{1,4},{2,5},{3,6},{4,7},{5,0},{6,1},{7,2},{8,11},{9,12},{10,... | collective-permute-start | bytes 589832 | tf_op jit(solution)/shard_map/ppermute | solution.py:27
  202.3 30.7 %collective-permute-start.3 = (bf16[1,24,4096]{2,1,0:T(8,128)(2,1)S(1)}, bf16[1,24,4096]{2,1,0:T(8,128)(2,1)S(1)}, u32[]{:S(2)}, u32[]{:S(2)}) collective-permute-start(bf16[1,24,4096]{2,1,0:T(8,128)(2,1)S(1)} %get-tuple-element.7), channel_id=1, source_target_pairs={{0,4},{1,5},{2,6},{3,7},{4,0},{5,1},{6,2},{7,3},{8,12},{9,13},{10,... | collective-permute-start | bytes 589832 | tf_op jit(solution)/shard_map/ppermute | solution.py:27
  203.6 29.5 %collective-permute-start.4 = (bf16[1,24,4096]{2,1,0:T(8,128)(2,1)S(1)}, bf16[1,24,4096]{2,1,0:T(8,128)(2,1)S(1)}, u32[]{:S(2)}, u32[]{:S(2)}) collective-permute-start(bf16[1,24,4096]{2,1,0:T(8,128)(2,1)S(1)} %get-tuple-element.6), channel_id=1, source_target_pairs={{0,5},{1,6},{2,7},{3,0},{4,1},{5,2},{6,3},{7,4},{8,13},{9,14},{10,... | collective-permute-start | bytes 589832 | tf_op jit(solution)/shard_map/ppermute | solution.py:27
  204.7 31.3 %collective-permute-start.5 = (bf16[1,24,4096]{2,1,0:T(8,128)(2,1)S(1)}, bf16[1,24,4096]{2,1,0:T(8,128)(2,1)S(1)}, u32[]{:S(2)}, u32[]{:S(2)}) collective-permute-start(bf16[1,24,4096]{2,1,0:T(8,128)(2,1)S(1)} %get-tuple-element.5), channel_id=1, source_target_pairs={{0,6},{1,7},{2,0},{3,1},{4,2},{5,3},{6,4},{7,5},{8,14},{9,15},{10,... | collective-permute-start | bytes 589832 | tf_op jit(solution)/shard_map/ppermute | solution.py:27
  208.7 28.5 %collective-permute-start.6 = (bf16[1,24,4096]{2,1,0:T(8,128)(2,1)S(1)}, bf16[1,24,4096]{2,1,0:T(8,128)(2,1)S(1)}, u32[]{:S(2)}, u32[]{:S(2)}) collective-permute-start(bf16[1,24,4096]{2,1,0:T(8,128)(2,1)S(1)} %get-tuple-element.4), channel_id=1, source_target_pairs={{0,7},{1,0},{2,1},{3,2},{4,3},{5,4},{6,5},{7,6},{8,15},{9,8},{10,9... | collective-permute-start | bytes 589832 | tf_op jit(solution)/shard_map/ppermute | solution.py:27
  233.0 7.4 %copy-start.4 = (s32[128]{0:T(128)S(1)}, s32[128]{0:T(128)}, u32[]{:S(2)}) copy-start(s32[128]{0:T(128)} %copy-done.3) | copy-start | bytes 1540
  237.2 1.2 copy-start.1
Sparse Core Ops, SparseCore 0:
  48.9 48.9 all-gather.1
  138.4 58.6 reduce-scatter.1
